TPU v7x, 128 devices: a whole 4x4x4 slice. The times are simulated.
128 devices in a mesh: vv: 16 (over z, x), oo: 8 (over y, core).
Axes of the slice: x: 4, y: 4, z: 4, core: 2. Of those that a mesh axis runs over, the one named last changes fastest.
Arguments:
- integrals: bfloat16 [32768, 20480], P('vv', 'oo'), may hold values from -0.0390625 to 0.0390625
- t2: bfloat16 [8, 20480, 1280], P(None, 'oo', 'vv'), may hold values from -6 to 6
- block_owner: int32 [16], replicated, may hold values from 0 to 7, as said below
Outputs:
- residual: float32 [32768, 1280], P('vv', 'oo')
Inputs may be any that keep to these rules, and one draw needn't show every extreme that they name: `block_owner`: each pair irrep 0 to 7 is named by exactly 2 row blocks.
All inputs are finite; a program needn't handle non-finite values.
Results may differ from a plain program's by a relative error of at most 0.0003.
Values may be sent and summed in bfloat16 or wider, within the bound.
A program may use at most 128 MiB of HBM per device.

v0:
```python
import jax
import jax.numpy as jnp
from jax import lax
from jax.sharding import PartitionSpec as P


def local(integrals, t2, block_owner):
    outgoing = t2[block_owner]
    partial_value = jnp.einsum(
        "rd,sdj->rsj",
        integrals,
        lax.all_to_all(outgoing, "vv", split_axis=0, concat_axis=0, tiled=True),
        preferred_element_type=jnp.float32,
    )
    partial_value = partial_value.reshape(
        partial_value.shape[0], partial_value.shape[1] * partial_value.shape[2]
    )
    return lax.psum_scatter(partial_value, "oo", scatter_dimension=1, tiled=True)


def solution(mesh):
    in_specs = (P("vv", "oo"), P(None, "oo", "vv"), P())
    out_specs = P("vv", "oo")
    return jax.shard_map(local, mesh=mesh, in_specs=in_specs, out_specs=out_specs, check_vma=False)
```

profile of v0, /device:TPU:1, one launch (start us, length us, event | category | flops | bytes accessed | tf_op | source)
XLA Modules:
  0.0 180.2 jit_solution(3035724919152235005)
XLA Ops:
  6.5 0.0 copy-start
  6.5 0.0 reduce-scatter.2.cloned.1.call-start
  6.5 0.8 compare_select_fusion
  7.4 1.1 copy-done
  8.5 3.7 %gather_fusion = bf16[16,2560,80]{1,2,0:T(8,128)(2,1)} fusion(bf16[8,2560,80]{1,2,0:T(8,128)(2,1)S(1)} %copy-done, s32[1024]{0:T(1024)S(1)} %pad_clamp_fusion), kind=kCustom, calls=%fused_computation | custom fusion | bytes 13107264 | tf_op jit(solution)/shard_map/gather | solution.py:8
  12.2 0.0 copy-start.1
  12.2 84.0 %all_to_all.5 = bf16[16,2560,80]{1,2,0:T(8,128)(2,1)S(1)} all-to-all(bf16[16,2560,80]{1,2,0:T(8,128)(2,1)} %gather_fusion), channel_id=1, replica_groups=mesh['vv'=16,'oo'=8] {'vv'}, dimensions={0} | all-to-all | bytes 13107200 | tf_op jit(solution)/shard_map/all_to_all | solution.py:12
  96.2 0.0 copy-done.1
  96.2 16.4 %fusion = f32[16,80,2048]{2,1,0:T(8,128)} fusion(bf16[16,2560,80]{1,2,0:T(8,128)(2,1)S(1)} %all_to_all.5, bf16[2048,2560]{1,0:T(8,128)(2,1)S(1)} %copy-done.1), kind=kOutput, calls=%fused_computation.1 | convolution fusion | flops 13421772800 | bytes 27525120 | tf_op jit(solution)/shard_map/rd,sdj->rsj/dot_general | solution.py:9
  112.6 0.0 reduce-scatter.2.cloned.1.call-update
  112.6 60.8 %reduce-scatter.2.cloned.1.call-done = f32[2048,160]{0,1:T(8,128)} async-done(((f32[2048,1280]{0,1:T(8,128)}), f32[2048,160]{0,1:T(8,128)}) %reduce-scatter.2.cloned.1.call-update) | async-done | bytes 1310736 | tf_op jit(solution)/shard_map/reduce_scatter | solution.py:18
  (1 shorter events, 0.0 us)
Async XLA Ops:
  6.5 1.9 %copy-start = (bf16[8,2560,80]{1,2,0:T(8,128)(2,1)S(1)}, bf16[8,2560,80]{1,2,0:T(8,128)(2,1)}, u32[]{:S(2)}) copy-start(bf16[8,2560,80]{1,2,0:T(8,128)(2,1)} %param.4) | copy-start | bytes 9830404
  6.5 166.8 %reduce-scatter.2.cloned.1.call-start = ((), (), s32[]{:S(2)}) async-start(), calls=%async_computation.2 | async-start | bytes 11796480 | tf_op jit(solution)/shard_map/reduce_scatter | solution.py:18
  12.2 84.0 %copy-start.1 = (bf16[2048,2560]{1,0:T(8,128)(2,1)S(1)}, bf16[2048,2560]{1,0:T(8,128)(2,1)}, u32[]{:S(2)}) copy-start(bf16[2048,2560]{1,0:T(8,128)(2,1)} %param.3) | copy-start | bytes 31457284
Sparse Core Ops, SparseCore 0:
  112.7 60.5 reduce-scatter.1
where the time goes:
time: 180 us
  blocking collectives  84 us (47%)
  waiting for transfers between devices  60.8 us (34%)
  matrix products  16.4 us (9%)
  between operations  13.4 us (7%)
  local copies, waits for them, and re-layouts  4.83 us (3%)
    all_to_all x1, blocking collectives, local(): lax.all_to_all(outgoing, 'vv', split_axis=0, concat_axis=0, tiled=True)  84 us
    reduce_scatter x1, waiting for transfers between devices, local(): lax.psum_scatter(partial_value, 'oo', scatter_dimension=1, tiled=True)  60.8 us
    dot_general x1, matrix products, local(): jnp.einsum('rd,sdj->rsj', integrals, lax.all_to_all(outgoing, 'vv', split...  16.4 us
    gather x1, local copies, waits for them, and re-layouts, local(): outgoing = t2[block_owner]  3.7 us
  transfers between devices with their start and end apart: 1, of which 1 were waited for; matrix products, arithmetic and copies ran while one was open for 0% of the time, Pallas kernels for 0%

commit v1 on v0

v1 whole, which is shorter than its diff:
```python
import functools

import jax
import jax.numpy as jnp
from jax import lax
from jax.experimental import pallas as pl
from jax.experimental.pallas import tpu as pltpu
from jax.sharding import PartitionSpec as P

MESH = pl.DeviceIdType.MESH
ROUNDS = (16, 16, 16, 16, 16)
NCH = 4
RHS_T = (((1,), (1,)), ((), ()))


def wrap(i):
    return lax.rem(i, 4)


def kernel(rounds, owner, a_hbm, t_hbm, o_hbm, *scratch):
    R = len(rounds)
    scratch = list(scratch)

    def take(n):
        got = scratch[:n]
        del scratch[:n]
        return got

    (a,) = take(1)
    t2v, snd, arr, fin, ra, rb, part, xin, yr, yin, out = (take(R) for _ in range(11))
    a_sem, t_sem, o_sem, sA, rA, sB, rB, sX, rX, sY, rY = take(11)
    CH = a.shape[0] // NCH
    offs = [sum(rounds[:r]) for r in range(R)]

    v, o = lax.axis_index("vv"), lax.axis_index("oo")
    z, x, y, c = lax.div(v, 4), wrap(v), lax.div(o, 2), lax.rem(o, 2)
    f, s = z * (1 - c) + x * c, x * (1 - c) + z * c

    def plane(ff, ss):
        return ff * (4 - 3 * c) + ss * (1 + 3 * c)

    def dev_a(d):
        return (plane(wrap(f + d), s), o)

    def dev_b(d):
        return (plane(f, wrap(s + d)), o)

    def dev_y(d):
        return (v, wrap(y + d) * 2 + c)

    sibling = (v, y * 2 + 1 - c)

    def load_t(r):
        return pltpu.make_async_copy(t_hbm.at[:, pl.ds(offs[r], rounds[r]), :], t2v[r], t_sem.at[r])

    def load_a(i):
        rows = pl.ds(i * CH, CH)
        return pltpu.make_async_copy(a_hbm.at[rows], a.at[rows], a_sem.at[i])

    for r in range(R):
        load_t(r).start()
    for i in range(NCH):
        load_a(i).start()

    barrier = pltpu.get_barrier_semaphore()
    peers = [dev_a(1), dev_a(3), dev_b(1), dev_b(3), dev_y(1), dev_y(3), sibling]
    for peer in peers:
        pl.semaphore_signal(barrier, inc=1, device_id=peer, device_id_type=MESH)
    pl.semaphore_wait(barrier, len(peers))

    def send(src, dst, ss, rs, to):
        return pltpu.make_async_remote_copy(
            src_ref=src, dst_ref=dst, send_sem=ss, recv_sem=rs, device_id=to, device_id_type=MESH
        )

    def A(r, i):
        src, dst, d = [
            (snd[r].at[2, 0:2], ra[r].at[0], 1),
            (snd[r].at[2, 2:4], ra[r].at[1], 3),
            (snd[r].at[1], arr[r].at[1], 1),
            (snd[r].at[3], arr[r].at[3], 3),
            (ra[r].at[0], arr[r].at[2, 0:2], 1),
            (ra[r].at[1], arr[r].at[2, 2:4], 3),
        ][i]
        return send(src, dst, sA.at[r, i], rA.at[r, i], dev_a(d))

    def B(r, i):
        src, dst, d = [
            (snd[r].at[0, 2], rb[r].at[0, 0], 1),
            (snd[r].at[0, 1], fin[r].at[1, 0], 1),
            (snd[r].at[0, 3], fin[r].at[3, 0], 3),
            (arr[r].at[1, 2], rb[r].at[0, 1], 1),
            (arr[r].at[2:4, 2], rb[r].at[1], 3),
            (arr[r].at[1:4, 1], fin[r].at[1, 1:4], 1),
            (arr[r].at[1:4, 3], fin[r].at[3, 1:4], 3),
            (rb[r].at[0], fin[r].at[2, 0:2], 1),
            (rb[r].at[1], fin[r].at[2, 2:4], 3),
        ][i]
        return send(src, dst, sB.at[r, i], rB.at[r, i], dev_b(d))

    def X(r, ch):
        return send(part[r].at[ch, 1 - c], xin[r].at[ch], sX.at[r, ch], rX.at[r, ch], sibling)

    def Y(r, ch, i):
        src, dst, d = [
            (part[r].at[ch, c, wrap(y + 2), 0], yr[r].at[ch, 0], 1),
            (part[r].at[ch, c, wrap(y + 2), 1], yr[r].at[ch, 1], 3),
            (part[r].at[ch, c, wrap(y + 1)], yin[r].at[ch, 0], 1),
            (part[r].at[ch, c, wrap(y + 3)], yin[r].at[ch, 1], 3),
        ][i]
        return send(src, dst, sY.at[r, ch, i], rY.at[r, ch, i], dev_y(d))

    def prep(r):
        load_t(r).wait()
        for j in (2, 1, 3, 0):
            for t in range(4):
                block = t2v[r][owner[plane(wrap(f + j), wrap(s + t))]]
                if j == 0 and t == 0:
                    fin[r][0, 0] = block
                else:
                    snd[r][j, t] = block

    def multiply(r, ch):
        u = rounds[r]
        left = fin[r][...].reshape(16 * u, fin[r].shape[-1])
        rows = pl.ds(pl.multiple_of(ch * CH, CH), CH)
        res = lax.dot_general(left, a[rows, :], RHS_T, preferred_element_type=jnp.float32)
        for t in range(4):
            for j in range(4):
                ff, ss = wrap(f - j + 4), wrap(s - t + 4)
                zs, xs = ff * (1 - c) + ss * c, ss * (1 - c) + ff * c
                i = 4 * t + j
                part[r][ch, lax.div(xs, 2), zs, lax.rem(xs, 2)] = res[i * u : (i + 1) * u]
        X(r, ch).start()

    def chip_sum(r, ch):
        X(r, ch).wait_recv()
        part[r][ch, c] = part[r][ch, c] + xin[r][ch]
        Y(r, ch, 0).start()
        Y(r, ch, 1).start()

    def compute(r):
        for i in (1, 2, 5, 6, 7, 8):
            B(r, i).wait_recv()
        for j in (1, 2, 3):
            fin[r][0, j] = arr[r][j, 0]
        if r == 0:
            for i in range(NCH):
                load_a(i).wait()

        multiply(r, 0)

        @pl.loop(1, NCH)
        def _(ch):
            multiply(r, ch)
            chip_sum(r, ch - 1)

        chip_sum(r, NCH - 1)

    def relay_y(r):
        @pl.loop(0, NCH)
        def _(ch):
            for i in range(2):
                d = wrap(y + 1 + 2 * i)
                Y(r, ch, i).wait_recv()
                part[r][ch, c, d, i] = part[r][ch, c, d, i] + yr[r][ch, i]
                Y(r, ch, 2 + i).start()

    def store(r, h):
        return pltpu.make_async_copy(out[r].at[h], o_hbm.at[pl.ds(80 * h + offs[r], rounds[r]), :], o_sem.at[r, h])

    def finish(r):
        @pl.loop(0, NCH)
        def _(ch):
            Y(r, ch, 2).wait_recv()
            Y(r, ch, 3).wait_recv()
            cols = pl.ds(pl.multiple_of(ch * CH, CH), CH)
            out[r][:, :, cols] = part[r][ch, c, y] + yin[r][ch, 0] + yin[r][ch, 1]

        for h in range(2):
            store(r, h).start()

    prep(0)
    for k in range(-1, R + 3):
        if k + 1 < R:
            for i in range(4):
                A(k + 1, i).start()
            for i in range(3):
                B(k + 1, i).start()
        if k + 2 < R:
            prep(k + 2)
        if 0 <= k < R:
            for i in (2, 3, 4, 5):
                A(k, i).wait_recv()
            for i in (3, 4, 5, 6):
                B(k, i).start()
        if k + 1 < R:
            for i in range(2):
                A(k + 1, i).wait_recv()
                A(k + 1, 4 + i).start()
        if 0 <= k - 2 < R:
            relay_y(k - 2)
        if 0 <= k < R:
            B(k, 0).wait_recv()
            B(k, 3).wait_recv()
            B(k, 7).start()
            B(k, 4).wait_recv()
            B(k, 8).start()
        if 0 <= k - 3 < R:
            finish(k - 3)
        if 0 <= k - 1 < R:
            compute(k - 1)

    for r in range(R):
        for i in range(6):
            A(r, i).wait_send()
        for i in range(9):
            B(r, i).wait_send()
        for h in range(2):
            store(r, h).wait()

        @pl.loop(0, NCH)
        def _(ch):
            X(r, ch).wait_send()
            for i in range(4):
                Y(r, ch, i).wait_send()


def local(integrals, t2, block_owner):
    t2 = jnp.swapaxes(t2, 1, 2)
    groups, width, depth = t2.shape
    rows = integrals.shape[0]
    R, ch = len(ROUNDS), rows // NCH
    bf16, f32 = jnp.bfloat16, jnp.float32

    def each(shape, dtype):
        return [pltpu.VMEM(shape(u), dtype) for u in ROUNDS]

    scratch = (
        [pltpu.VMEM((rows, depth), bf16)]
        + each(lambda u: (groups, u, depth), bf16)
        + each(lambda u: (4, 4, u, depth), bf16)
        + each(lambda u: (4, 4, u, depth), bf16)
        + each(lambda u: (4, 4, u, depth), bf16)
        + each(lambda u: (2, 2, u, depth), bf16)
        + each(lambda u: (2, 2, u, depth), bf16)
        + each(lambda u: (NCH, 2, 4, 2, u, ch), f32)
        + each(lambda u: (NCH, 4, 2, u, ch), f32)
        + each(lambda u: (NCH, 2, u, ch), f32)
        + each(lambda u: (NCH, 2, 2, u, ch), f32)
        + each(lambda u: (2, u, rows), f32)
        + [
            pltpu.SemaphoreType.DMA((NCH,)),
            pltpu.SemaphoreType.DMA((R,)),
            pltpu.SemaphoreType.DMA((R, 2)),
            pltpu.SemaphoreType.DMA((R, 6)),
            pltpu.SemaphoreType.DMA((R, 6)),
            pltpu.SemaphoreType.DMA((R, 9)),
            pltpu.SemaphoreType.DMA((R, 9)),
            pltpu.SemaphoreType.DMA((R, NCH)),
            pltpu.SemaphoreType.DMA((R, NCH)),
            pltpu.SemaphoreType.DMA((R, NCH, 4)),
            pltpu.SemaphoreType.DMA((R, NCH, 4)),
        ]
    )
    result = pl.pallas_call(
        functools.partial(kernel, ROUNDS),
        name="ladder",
        out_shape=jax.ShapeDtypeStruct((2 * width, rows), f32),
        in_specs=[
            pl.BlockSpec(memory_space=pltpu.SMEM),
            pl.BlockSpec(memory_space=pl.ANY),
            pl.BlockSpec(memory_space=pl.ANY),
        ],
        out_specs=pl.BlockSpec(memory_space=pl.ANY),
        scratch_shapes=scratch,
        compiler_params=pltpu.CompilerParams(collective_id=0, has_side_effects=True, vmem_limit_bytes=66_500_000),
    )(block_owner, integrals, t2)
    return result.T


def solution(mesh):
    in_specs = (P("vv", "oo"), P(None, "oo", "vv"), P())
    return jax.shard_map(local, mesh=mesh, in_specs=in_specs, out_specs=P("vv", "oo"), check_vma=False)
```

time: 180 us -> 109 us (0.61)
  Pallas kernels: 0 us -> 107 us
  blocking collectives: 84 us -> 0 us
  waiting for transfers between devices: 60.8 us -> 0 us
  matrix products: 16.4 us -> 0 us
  between operations: 13.4 us -> 0.01 us
  local copies, waits for them, and re-layouts: 4.83 us -> 2.5 us
    pallas_call x0 -> x1, Pallas kernels: none -> 107 us  [local(): pl.pallas_call(functools.partial(kernel, ROUNDS), name='ladder', out_shap...]
    all_to_all x1 -> x0, blocking collectives: 84 us -> none  [local(): lax.all_to_all(outgoing, 'vv', split_axis=0, concat_axis=0, tiled=True)]
    reduce_scatter x1 -> x0, waiting for transfers between devices: 60.8 us -> none  [local(): lax.psum_scatter(partial_value, 'oo', scatter_dimension=1, tiled=True)]
    dot_general x1 -> x0, matrix products: 16.4 us -> none  [local(): jnp.einsum('rd,sdj->rsj', integrals, lax.all_to_all(outgoing, 'vv', split...]
    gather x1 -> x0, local copies, waits for them, and re-layouts: 3.7 us -> none  [local(): outgoing = t2[block_owner]]
  transfers between devices with their start and end apart: 1 -> 0, of which waited for: 1 -> 0; matrix products, arithmetic and copies ran while one was open for 0% -> 0% of each run, Pallas kernels for 0% -> 0%
where the time goes in v1:
time: 109 us
  Pallas kernels  107 us (98%)
  local copies, waits for them, and re-layouts  2.5 us (2%)
    pallas_call x1, Pallas kernels, local(): pl.pallas_call(functools.partial(kernel, ROUNDS), name='ladder', out_shap...  107 us
    unnamed x1, local copies, waits for them, and re-layouts  2.5 us

profile of v1, /device:TPU:1, one launch (start us, length us, event | category | flops | bytes accessed | tf_op | source)
XLA Modules:
  0.0 109.2 jit_solution(12075487416679509244)
XLA Ops:
  0.0 106.7 %ladder.1 = f32[160,2048]{1,0:T(8,128)} custom-call(s32[16]{0:T(128)} %owner.1, bf16[2048,2560]{1,0:T(8,128)(2,1)} %a_hbm.1, bf16[8,80,2560]{2,1,0:T(8,128)(2,1)} %bitcast.3), custom_call_target="tpu_custom_call" | custom-call | tf_op jit(solution)/shard_map/ladder/pallas_call | solution.py:266
  106.7 2.5 %copy.5 = f32[2048,160]{0,1:T(8,128)} copy(f32[2048,160]{0,1:T(8,128)} %bitcast.2) | data formatting | bytes 2621440

commit v2 on v1

--- a/solution.py
+++ b/solution.py
@@ -9,7 +9,8 @@
 
 MESH = pl.DeviceIdType.MESH
 ROUNDS = (16, 16, 16, 16, 16)
-NCH = 4
+NCH = 2
+FULL = 32000.0
 RHS_T = (((1,), (1,)), ((), ()))
 
 
@@ -17,7 +18,22 @@
     return lax.rem(i, 4)
 
 
-def kernel(rounds, owner, a_hbm, t_hbm, o_hbm, *scratch):
+def encode(ref, value):
+    width = value.shape[-1]
+    most = jnp.maximum(jnp.max(jnp.abs(value), axis=-1, keepdims=True), 1e-30)
+    power = jnp.ceil(jnp.log2(most))
+    scale = FULL * jnp.exp2(-power)
+    ref[:, 0:width] = jnp.round(value * scale).astype(jnp.int16)
+    ref[:, width : width + 128] = jnp.broadcast_to(power, (value.shape[0], 128)).astype(jnp.int16)
+
+
+def decode(code):
+    width = code.shape[-1] - 128
+    power = code[:, width : width + 1].astype(jnp.float32)
+    return code[:, 0:width].astype(jnp.float32) * (jnp.exp2(power) * (1.0 / FULL))
+
+
+def kernel(rounds, owner, a_hbm, t_hbm, o_ref, *scratch):
     R = len(rounds)
     scratch = list(scratch)
 
@@ -27,8 +43,8 @@
         return got
 
     (a,) = take(1)
-    t2v, snd, arr, fin, ra, rb, part, xin, yr, yin, out = (take(R) for _ in range(11))
-    a_sem, t_sem, o_sem, sA, rA, sB, rB, sX, rX, sY, rY = take(11)
+    t2v, snd, arr, fin, ra, rb, part, xin, q1, q2, yr, yin = (take(R) for _ in range(12))
+    a_sem, t_sem, sA, rA, sB, rB, sX, rX, sY, rY = take(10)
     CH = a.shape[0] // NCH
     offs = [sum(rounds[:r]) for r in range(R)]
 
@@ -103,10 +119,10 @@
 
     def Y(r, ch, i):
         src, dst, d = [
-            (part[r].at[ch, c, wrap(y + 2), 0], yr[r].at[ch, 0], 1),
-            (part[r].at[ch, c, wrap(y + 2), 1], yr[r].at[ch, 1], 3),
-            (part[r].at[ch, c, wrap(y + 1)], yin[r].at[ch, 0], 1),
-            (part[r].at[ch, c, wrap(y + 3)], yin[r].at[ch, 1], 3),
+            (q1[r].at[ch, 0], yr[r].at[ch, 0], 1),
+            (q1[r].at[ch, 1], yr[r].at[ch, 1], 3),
+            (q2[r].at[ch, 0], yin[r].at[ch, 0], 1),
+            (q2[r].at[ch, 1], yin[r].at[ch, 1], 3),
         ][i]
         return send(src, dst, sY.at[r, ch, i], rY.at[r, ch, i], dev_y(d))
 
@@ -136,6 +152,9 @@
     def chip_sum(r, ch):
         X(r, ch).wait_recv()
         part[r][ch, c] = part[r][ch, c] + xin[r][ch]
+        far = part[r][ch, c, wrap(y + 2)]
+        for h in range(2):
+            encode(q1[r].at[ch, h], far[h])
         Y(r, ch, 0).start()
         Y(r, ch, 1).start()
 
@@ -162,12 +181,11 @@
         def _(ch):
             for i in range(2):
                 d = wrap(y + 1 + 2 * i)
+                near = part[r][ch, c, d]
                 Y(r, ch, i).wait_recv()
-                part[r][ch, c, d, i] = part[r][ch, c, d, i] + yr[r][ch, i]
+                encode(q2[r].at[ch, i, i], near[i] + decode(yr[r][ch, i]))
+                encode(q2[r].at[ch, i, 1 - i], near[1 - i])
                 Y(r, ch, 2 + i).start()
-
-    def store(r, h):
-        return pltpu.make_async_copy(out[r].at[h], o_hbm.at[pl.ds(80 * h + offs[r], rounds[r]), :], o_sem.at[r, h])
 
     def finish(r):
         @pl.loop(0, NCH)
@@ -175,10 +193,9 @@
             Y(r, ch, 2).wait_recv()
             Y(r, ch, 3).wait_recv()
             cols = pl.ds(pl.multiple_of(ch * CH, CH), CH)
-            out[r][:, :, cols] = part[r][ch, c, y] + yin[r][ch, 0] + yin[r][ch, 1]
-
-        for h in range(2):
-            store(r, h).start()
+            for h in range(2):
+                rows = pl.ds(80 * h + offs[r], rounds[r])
+                o_ref[rows, cols] = part[r][ch, c, y, h] + decode(yin[r][ch, 0, h]) + decode(yin[r][ch, 1, h])
 
     prep(0)
     for k in range(-1, R + 3):
@@ -216,8 +233,6 @@
             A(r, i).wait_send()
         for i in range(9):
             B(r, i).wait_send()
-        for h in range(2):
-            store(r, h).wait()
 
         @pl.loop(0, NCH)
         def _(ch):
@@ -246,13 +261,13 @@
         + each(lambda u: (2, 2, u, depth), bf16)
         + each(lambda u: (NCH, 2, 4, 2, u, ch), f32)
         + each(lambda u: (NCH, 4, 2, u, ch), f32)
-        + each(lambda u: (NCH, 2, u, ch), f32)
-        + each(lambda u: (NCH, 2, 2, u, ch), f32)
-        + each(lambda u: (2, u, rows), f32)
+        + each(lambda u: (NCH, 2, u, ch + 128), jnp.int16)
+        + each(lambda u: (NCH, 2, 2, u, ch + 128), jnp.int16)
+        + each(lambda u: (NCH, 2, u, ch + 128), jnp.int16)
+        + each(lambda u: (NCH, 2, 2, u, ch + 128), jnp.int16)
         + [
             pltpu.SemaphoreType.DMA((NCH,)),
             pltpu.SemaphoreType.DMA((R,)),
-            pltpu.SemaphoreType.DMA((R, 2)),
             pltpu.SemaphoreType.DMA((R, 6)),
             pltpu.SemaphoreType.DMA((R, 6)),
             pltpu.SemaphoreType.DMA((R, 9)),
@@ -266,15 +281,15 @@
     result = pl.pallas_call(
         functools.partial(kernel, ROUNDS),
         name="ladder",
-        out_shape=jax.ShapeDtypeStruct((2 * width, rows), f32),
+        out_shape=pltpu.VMEM((2 * width, rows), f32),
         in_specs=[
             pl.BlockSpec(memory_space=pltpu.SMEM),
             pl.BlockSpec(memory_space=pl.ANY),
             pl.BlockSpec(memory_space=pl.ANY),
         ],
-        out_specs=pl.BlockSpec(memory_space=pl.ANY),
+        out_specs=pl.BlockSpec(memory_space=pltpu.VMEM),
         scratch_shapes=scratch,
-        compiler_params=pltpu.CompilerParams(collective_id=0, has_side_effects=True, vmem_limit_bytes=66_500_000),
+        compiler_params=pltpu.CompilerParams(collective_id=0, has_side_effects=True, vmem_limit_bytes=65_000_000),
     )(block_owner, integrals, t2)
     return result.T
 

time: 109 us -> 104 us (0.954)
  Pallas kernels: 107 us -> 102 us
  local copies, waits for them, and re-layouts: 2.5 us -> 1.06 us
    pallas_call x1, Pallas kernels: 107 us -> 102 us  [local(): pl.pallas_call(functools.partial(kernel, ROUNDS), name='ladder', out_shap...]
    unnamed x1, local copies, waits for them, and re-layouts: 2.5 us -> 1.06 us
where the time goes in v2:
time: 104 us; the launch traced here: 103 us
  Pallas kernels  102 us (98%)
  local copies, waits for them, and re-layouts  1.06 us (1%)
    pallas_call x1, Pallas kernels, local(): pl.pallas_call(functools.partial(kernel, ROUNDS), name='ladder', out_shap...  102 us

profile of v2, /device:TPU:1, one launch (start us, length us, event | category | flops | bytes accessed | tf_op | source)
XLA Modules:
  0.0 103.3 jit_solution(2420983538931803299)
XLA Ops:
  0.0 102.2 %ladder.1 = f32[160,2048]{1,0:T(8,128)S(1)} custom-call(s32[16]{0:T(128)} %owner.1, bf16[2048,2560]{1,0:T(8,128)(2,1)} %a_hbm.1, bf16[8,80,2560]{2,1,0:T(8,128)(2,1)} %bitcast.3), custom_call_target="tpu_custom_call" | custom-call | tf_op jit(solution)/shard_map/ladder/pallas_call | solution.py:281
  102.2 1.1 %copy.5 = f32[2048,160]{0,1:T(8,128)} copy(f32[2048,160]{0,1:T(8,128)S(1)} %bitcast.2) | data formatting | bytes 2621440

commit v3 on v2

--- a/solution.py
+++ b/solution.py
@@ -8,7 +8,7 @@
 from jax.sharding import PartitionSpec as P
 
 MESH = pl.DeviceIdType.MESH
-ROUNDS = (16, 16, 16, 16, 16)
+ROUNDS = (24, 24, 16, 16)
 NCH = 2
 FULL = 32000.0
 RHS_T = (((1,), (1,)), ((), ()))
@@ -73,10 +73,7 @@
         rows = pl.ds(i * CH, CH)
         return pltpu.make_async_copy(a_hbm.at[rows], a.at[rows], a_sem.at[i])
 
-    for r in range(R):
-        load_t(r).start()
-    for i in range(NCH):
-        load_a(i).start()
+    load_t(0).start()
 
     barrier = pltpu.get_barrier_semaphore()
     peers = [dev_a(1), dev_a(3), dev_b(1), dev_b(3), dev_y(1), dev_y(3), sibling]
@@ -204,6 +201,11 @@
                 A(k + 1, i).start()
             for i in range(3):
                 B(k + 1, i).start()
+        if k == -1:
+            for r in range(1, R):
+                load_t(r).start()
+            for i in range(NCH):
+                load_a(i).start()
         if k + 2 < R:
             prep(k + 2)
         if 0 <= k < R:

time: 104 us -> 103 us (level)
  no operation moved by 1% of the time
where the time goes in v3:
time: 103 us
  Pallas kernels  102 us (99%)
  local copies, waits for them, and re-layouts  1.06 us (1%)
    pallas_call x1, Pallas kernels, local(): pl.pallas_call(functools.partial(kernel, ROUNDS), name='ladder', out_shap...  102 us

profile of v3, /device:TPU:1, one launch (start us, length us, event | category | flops | bytes accessed | tf_op | source)
XLA Modules:
  0.0 103.0 jit_solution(1057957671178713317)
XLA Ops:
  0.0 101.9 %ladder.1 = f32[160,2048]{1,0:T(8,128)S(1)} custom-call(s32[16]{0:T(128)} %owner.1, bf16[2048,2560]{1,0:T(8,128)(2,1)} %a_hbm.1, bf16[8,80,2560]{2,1,0:T(8,128)(2,1)} %bitcast.3), custom_call_target="tpu_custom_call" | custom-call | tf_op jit(solution)/shard_map/ladder/pallas_call | solution.py:283
  101.9 1.1 %copy.5 = f32[2048,160]{0,1:T(8,128)} copy(f32[2048,160]{0,1:T(8,128)S(1)} %bitcast.2) | data formatting | bytes 2621440
